TPU v7x, 512 devices: a whole 4x8x8 slice. The times are simulated.
512 devices in a mesh: energy: 32 (over y, z_lo), atom: 16 (over x, z_hi, core).
Axes of the slice: x: 4, y: 8, z: 8 (z_hi: 2, z_lo: 4; z = z_hi * 4 + z_lo), core: 2. Of those that a mesh axis runs over, the one named last changes fastest.
Arguments:
- green_blocks: bfloat16 [256, 32, 2, 128, 128], P('atom', 'energy'), may hold values from -3 to 3
- coupling: bfloat16 [256, 3, 2, 128, 128], P('atom'), may hold values from -0.375 to 0.375
- phonon_weight: float32 [2, 256, 4], P(None, 'atom'), may hold values from 0.1 to 1
- offsets: int32 [256, 4], P('atom'), may hold values from 1 to 4, as said below
- bond_atom: int32 [256], P('atom'), may hold values from 0 to 127, as said below
Outputs:
- sigma: bfloat16 [128, 32, 2, 128, 128], P('atom', 'energy')
Inputs may be any that keep to these rules, and one draw needn't show every extreme that they name: For every bond, its 4 modes' offsets are 1, 2, 3 and 4 in some order. `bond_atom`: atoms k * 8 to (k + 1) * 8 - 1 lie on index k of atom. Among the 16 bonds of one index of atom, every index of atom that is named is named by exactly 2 bonds, and one index of atom is named by 2 bonds of every index of atom.
All inputs are finite; a program needn't handle non-finite values.
Results may differ from a plain program's by a relative error of at most 0.0064.
Values may be sent and summed in bfloat16 or wider, within the bound.
A program may use at most 64 MiB of HBM per device.

v0:
```python
import jax
import jax.numpy as jnp
from jax import lax
from jax.sharding import PartitionSpec as P

A_DEV = 8


def shifted(block, axis, distance):
    devices = range(lax.axis_size(axis))
    route = [((i - distance) % len(devices), i) for i in devices]
    return lax.ppermute(block, axis, route)


def window_mix(
    green_blocks, phonon_weight, offsets, mode_count, energy_count, bond_count, pieces_list
):
    span = len(pieces_list) * energy_count
    center = mode_count * energy_count
    local_energy = jnp.arange(energy_count, dtype=jnp.int32)
    window_slots = jnp.arange(span, dtype=jnp.int32)
    lower_pos = center + local_energy[None, :, None] - offsets[:, None, :]
    upper_pos = center + local_energy[None, :, None] + offsets[:, None, :]
    lower_hit = (lower_pos[..., None] == window_slots).astype(jnp.float32)
    upper_hit = (upper_pos[..., None] == window_slots).astype(jnp.float32)
    absorb = phonon_weight[0][:, None, :, None]
    emit = phonon_weight[1][:, None, :, None]
    coefficient = jnp.sum(absorb * lower_hit + emit * upper_hit, axis=2)
    mixed = jnp.zeros((bond_count, energy_count) + green_blocks.shape[2:], jnp.float32)
    for slot_number, window_piece in enumerate(pieces_list):
        weight_now = coefficient[:, :, slot_number * energy_count]
        mixed = mixed + weight_now[:, :, None, None, None] * window_piece[:, 0][:, None].astype(
            jnp.float32
        )
    return mixed.astype(jnp.bfloat16)


def body(green_blocks, coupling, phonon_weight, offsets, bond_atom):
    bond_count = green_blocks.shape[0]
    energy_count = green_blocks.shape[1]
    mode_count = offsets.shape[1]
    below_list = []
    above_list = []
    for distance in range(1, mode_count + 1):
        below_list.append(shifted(green_blocks, "energy", distance))
        above_list.append(shifted(green_blocks, "energy", -distance))
    pieces_list = below_list[::-1] + [green_blocks] + above_list
    mixed_half = window_mix(
        green_blocks, phonon_weight, offsets, mode_count, energy_count, bond_count, pieces_list
    )
    real_coupling = coupling[:, :, 0]
    imag_coupling = coupling[:, :, 1]
    real_mixed = mixed_half[:, :, 0]
    imag_mixed = mixed_half[:, :, 1]

    def left_mul(first, second):
        return jnp.einsum("bcij,bejk->becik", first, second, preferred_element_type=jnp.float32)

    def right_mul(first, second):
        return jnp.einsum("becij,bckj->beik", first, second, preferred_element_type=jnp.float32)

    left_real = (left_mul(real_coupling, real_mixed) - left_mul(imag_coupling, imag_mixed)).astype(
        jnp.bfloat16
    )
    left_imag = (left_mul(real_coupling, imag_mixed) + left_mul(imag_coupling, real_mixed)).astype(
        jnp.bfloat16
    )
    out_real = right_mul(left_real, real_coupling) - right_mul(left_imag, imag_coupling)
    out_imag = right_mul(left_real, imag_coupling) + right_mul(left_imag, real_coupling)
    bond_self = jnp.stack([out_real, out_imag], axis=2).astype(jnp.bfloat16)
    owner_count = lax.axis_size("atom")
    capacity = max(2, 2 * bond_count // owner_count)
    owner_index = bond_atom // A_DEV
    local_atom = bond_atom % A_DEV
    bond_order = jnp.arange(bond_count, dtype=jnp.int32)
    same_owner = (owner_index[None, :] == owner_index[:, None]) & (
        bond_order[None, :] < bond_order[:, None]
    )
    rank_index = jnp.sum(same_owner.astype(jnp.int32), axis=1)
    slot_index = owner_index * capacity + rank_index
    slot_count = owner_count * capacity
    slot_order = jnp.arange(slot_count, dtype=jnp.int32)
    slot_match = slot_index[None, :] == slot_order[:, None]
    outgoing = jnp.dot(
        slot_match.astype(jnp.bfloat16),
        bond_self.reshape(bond_count, -1),
        preferred_element_type=jnp.float32,
    )
    outgoing = outgoing.astype(jnp.bfloat16).reshape((owner_count, capacity) + bond_self.shape[1:])
    slot_atom = jnp.sum(jnp.where(slot_match, local_atom[None, :] + 1, 0), axis=1) - 1
    slot_atom = slot_atom.reshape(owner_count, capacity)
    incoming, arriving_atom = (
        lax.all_to_all(outgoing, "atom", split_axis=0, concat_axis=0, tiled=True),
        lax.all_to_all(slot_atom, "atom", split_axis=0, concat_axis=0, tiled=True),
    )
    collect = (
        arriving_atom.reshape(-1)[None, :] == jnp.arange(A_DEV, dtype=jnp.int32)[:, None]
    ).astype(jnp.bfloat16)
    sigma = jnp.dot(collect, incoming.reshape(slot_count, -1), preferred_element_type=jnp.float32)
    return sigma.reshape((A_DEV,) + bond_self.shape[1:]).astype(jnp.bfloat16)


def solution(mesh):
    placed = (
        P("atom", "energy", None, None, None),
        P("atom", None, None, None, None),
        P(None, "atom", None),
        P("atom", None),
        P("atom"),
    )
    return jax.shard_map(
        body,
        mesh=mesh,
        in_specs=placed,
        out_specs=P("atom", "energy", None, None, None),
        check_vma=False,
    )
```

profile of v0, /device:TPU:16, one launch (start us, length us, event | category | flops | bytes accessed | tf_op | source)
XLA Modules:
  0.0 287.5 jit_solution(17691319590824281355)
XLA Ops:
  0.0 1.7 copy.73
  1.7 3.5 %collective-permute-start = (bf16[16,1,2,128,128]{3,4,0,2,1:T(8,128)(2,1)S(1)}, bf16[16,1,2,128,128]{3,4,0,2,1:T(8,128)(2,1)S(1)}, u32[]{:S(2)}, u32[]{:S(2)}) collective-permute-start(bf16[16,1,2,128,128]{3,4,0,2,1:T(8,128)(2,1)S(1)} %copy.73), channel_id=1, source_target_pairs={{448,0},{464,16},{480,32},{496,48},{0,64},{16,80},{32,96},{48,112}... | collective-permute-start | bytes 3145736 | tf_op jit(solution)/shard_map/ppermute | solution.py:12
  5.2 7.9 %collective-permute-start.1 = (bf16[16,1,2,128,128]{3,4,0,2,1:T(8,128)(2,1)S(1)}, bf16[16,1,2,128,128]{3,4,0,2,1:T(8,128)(2,1)S(1)}, u32[]{:S(2)}, u32[]{:S(2)}) collective-permute-start(bf16[16,1,2,128,128]{3,4,0,2,1:T(8,128)(2,1)S(1)} %copy.73), channel_id=1, source_target_pairs={{464,0},{480,16},{496,32},{0,48},{16,64},{32,80},{48,96},{64,112},... | collective-permute-start | bytes 3145736 | tf_op jit(solution)/shard_map/ppermute | solution.py:12
  13.1 2.0 collective-permute-start.2
  15.1 4.3 %collective-permute-start.3 = (bf16[16,1,2,128,128]{3,4,0,2,1:T(8,128)(2,1)S(1)}, bf16[16,1,2,128,128]{3,4,0,2,1:T(8,128)(2,1)}, u32[]{:S(2)}, u32[]{:S(2)}) collective-permute-start(bf16[16,1,2,128,128]{3,4,0,2,1:T(8,128)(2,1)S(1)} %copy.73), channel_id=1, source_target_pairs={{496,0},{0,16},{16,32},{32,48},{48,64},{64,80},{80,96},{96,112},{1... | collective-permute-start | bytes 3145736 | tf_op jit(solution)/shard_map/ppermute | solution.py:12
  19.4 4.3 %collective-permute-start.4 = (bf16[16,1,2,128,128]{3,4,0,2,1:T(8,128)(2,1)S(1)}, bf16[16,1,2,128,128]{3,4,0,2,1:T(8,128)(2,1)}, u32[]{:S(2)}, u32[]{:S(2)}) collective-permute-start(bf16[16,1,2,128,128]{3,4,0,2,1:T(8,128)(2,1)S(1)} %copy.73), channel_id=1, source_target_pairs={{16,0},{32,16},{48,32},{64,48},{80,64},{96,80},{112,96},{128,112},... | collective-permute-start | bytes 3145736 | tf_op jit(solution)/shard_map/ppermute | solution.py:12
  23.8 4.6 %collective-permute-done = bf16[16,1,2,128,128]{3,4,0,2,1:T(8,128)(2,1)S(1)} collective-permute-done((bf16[16,1,2,128,128]{3,4,0,2,1:T(8,128)(2,1)S(1)}, bf16[16,1,2,128,128]{3,4,0,2,1:T(8,128)(2,1)S(1)}, u32[]{:S(2)}, u32[]{:S(2)}) %collective-permute-start) | collective-permute-done | bytes 1048608 | tf_op jit(solution)/shard_map/ppermute | solution.py:12
  28.5 7.1 %collective-permute-start.5 = (bf16[16,1,2,128,128]{3,4,0,2,1:T(8,128)(2,1)S(1)}, bf16[16,1,2,128,128]{3,4,0,2,1:T(8,128)(2,1)}, u32[]{:S(2)}, u32[]{:S(2)}) collective-permute-start(bf16[16,1,2,128,128]{3,4,0,2,1:T(8,128)(2,1)S(1)} %copy.73), channel_id=1, source_target_pairs={{32,0},{48,16},{64,32},{80,48},{96,64},{112,80},{128,96},{144,112}... | collective-permute-start | bytes 3145736 | tf_op jit(solution)/shard_map/ppermute | solution.py:12
  35.6 84.7 %collective-permute-done.1 = bf16[16,1,2,128,128]{3,4,0,2,1:T(8,128)(2,1)S(1)} collective-permute-done((bf16[16,1,2,128,128]{3,4,0,2,1:T(8,128)(2,1)S(1)}, bf16[16,1,2,128,128]{3,4,0,2,1:T(8,128)(2,1)S(1)}, u32[]{:S(2)}, u32[]{:S(2)}) %collective-permute-start.1) | collective-permute-done | bytes 1048608 | tf_op jit(solution)/shard_map/ppermute | solution.py:12
  120.3 1.9 collective-permute-start.6
  122.2 49.4 %collective-permute-done.2 = bf16[16,1,2,128,128]{3,4,0,2,1:T(8,128)(2,1)S(1)} collective-permute-done((bf16[16,1,2,128,128]{3,4,0,2,1:T(8,128)(2,1)S(1)}, bf16[16,1,2,128,128]{3,4,0,2,1:T(8,128)(2,1)S(1)}, u32[]{:S(2)}, u32[]{:S(2)}) %collective-permute-start.2) | collective-permute-done | bytes 1048608 | tf_op jit(solution)/shard_map/ppermute | solution.py:12
  171.6 1.0 copy-done.1
  172.6 1.9 collective-permute-start.7
  175.3 10.2 %all-to-all-start = ((s32[16,1,2]{2,1,0:T(1,128)}), s32[16,1,2]{2,1,0:T(1,128)S(1)}, u32[]{:S(2)}, u32[]{:S(2)}) async-start(s32[16,1,2]{2,1,0:T(1,128)} %bitcast), calls=%async_computation | async-start | bytes 16384 | tf_op jit(solution)/shard_map/all_to_all | solution.py:94
  185.6 7.2 %collective-permute-done.3 = bf16[16,1,2,128,128]{3,4,0,2,1:T(8,128)(2,1)} collective-permute-done((bf16[16,1,2,128,128]{3,4,0,2,1:T(8,128)(2,1)S(1)}, bf16[16,1,2,128,128]{3,4,0,2,1:T(8,128)(2,1)}, u32[]{:S(2)}, u32[]{:S(2)}) %collective-permute-start.3) | collective-permute-done | bytes 1048608 | tf_op jit(solution)/shard_map/ppermute | solution.py:12
  192.8 12.6 %collective-permute-done.5 = bf16[16,1,2,128,128]{3,4,0,2,1:T(8,128)(2,1)} collective-permute-done((bf16[16,1,2,128,128]{3,4,0,2,1:T(8,128)(2,1)S(1)}, bf16[16,1,2,128,128]{3,4,0,2,1:T(8,128)(2,1)}, u32[]{:S(2)}, u32[]{:S(2)}) %collective-permute-start.5) | collective-permute-done | bytes 1048608 | tf_op jit(solution)/shard_map/ppermute | solution.py:12
  205.4 4.5 %add_convert_fusion.1 = bf16[16,1,2,128,128]{3,4,0,2,1:T(8,128)(2,1)S(1)} fusion(bf16[16,1,2,128,128]{3,4,0,2,1:T(8,128)(2,1)} %collective-permute-done.7, bf16[16,1,2,128,128]{3,4,0,2,1:T(8,128)(2,1)} %collective-permute-done.6, bf16[16,1,2,128,128]{3,4,0,2,1:T(8,128)(2,1)} %collective-permute-done.5, ...), kind=kLoop, calls=%fused_computation.5 | loop fusion | flops 14155776 | bytes 10486336 | tf_op jit(solution)/shard_map/convert_element_type | solution.py:35
  210.6 0.8 fusion.7
  211.4 0.8 subtract_convert_fusion
  212.2 0.8 fusion.21
  213.0 0.8 add_convert_fusion
  213.8 0.8 fusion.26
  214.6 0.8 fusion.69
  215.4 0.8 fusion.64
  217.0 0.8 fusion.2
  217.8 1.8 copy.105
  219.6 10.1 %all-to-all-start.1 = ((bf16[16,2,1,2,128,128]{5,4,3,1,2,0:T(8,128)(2,1)}), bf16[16,2,1,2,128,128]{5,4,3,1,2,0:T(8,128)(2,1)S(1)}, u32[]{:S(2)}, u32[]{:S(2)}) async-start(bf16[16,2,1,2,128,128]{5,4,3,1,2,0:T(8,128)(2,1)} %bitcast.47), calls=%async_computation.1 | async-start | bytes 4194304 | tf_op jit(solution)/shard_map/all_to_all | solution.py:93
  231.0 50.1 %all-to-all-done.1 = bf16[16,2,1,2,128,128]{5,4,3,1,2,0:T(8,128)(2,1)S(1)} async-done(((bf16[16,2,1,2,128,128]{5,4,3,1,2,0:T(8,128)(2,1)}), bf16[16,2,1,2,128,128]{5,4,3,1,2,0:T(8,128)(2,1)S(1)}, u32[]{:S(2)}, u32[]{:S(2)}) %all-to-all-start.1) | async-done | bytes 2097184 | tf_op jit(solution)/shard_map/all_to_all | solution.py:93
  281.0 2.3 reshape.160
  283.3 2.1 copy.106
  285.4 1.2 fusion.74
  286.6 0.9 copy.91
  (30 shorter events, 3.8 us)
Async XLA Ops:
  0.0 23.6 %copy-start.4 = (s32[16]{0:T(128)S(1)}, s32[16]{0:T(128)}, u32[]{:S(2)}) copy-start(s32[16]{0:T(128)} %param.9) | copy-start | bytes 196
  0.0 185.5 %copy-start.2 = (f32[2,16,4]{1,2,0:T(4,128)S(1)}, f32[2,16,4]{1,2,0:T(4,128)}, u32[]{:S(2)}) copy-start(f32[2,16,4]{1,2,0:T(4,128)} %param.7) | copy-start | bytes 1540
  0.0 185.5 %copy-start.3 = (s32[16,4]{0,1:T(4,128)S(1)}, s32[16,4]{0,1:T(4,128)}, u32[]{:S(2)}) copy-start(s32[16,4]{0,1:T(4,128)} %param.8) | copy-start | bytes 772
  1.7 26.8 %collective-permute-start = (bf16[16,1,2,128,128]{3,4,0,2,1:T(8,128)(2,1)S(1)}, bf16[16,1,2,128,128]{3,4,0,2,1:T(8,128)(2,1)S(1)}, u32[]{:S(2)}, u32[]{:S(2)}) collective-permute-start(bf16[16,1,2,128,128]{3,4,0,2,1:T(8,128)(2,1)S(1)} %copy.73), channel_id=1, source_target_pairs={{448,0},{464,16},{480,32},{496,48},{0,64},{16,80},{32,96},{48,112}... | collective-permute-start | bytes 3145736 | tf_op jit(solution)/shard_map/ppermute | solution.py:12
  5.2 115.2 %collective-permute-start.1 = (bf16[16,1,2,128,128]{3,4,0,2,1:T(8,128)(2,1)S(1)}, bf16[16,1,2,128,128]{3,4,0,2,1:T(8,128)(2,1)S(1)}, u32[]{:S(2)}, u32[]{:S(2)}) collective-permute-start(bf16[16,1,2,128,128]{3,4,0,2,1:T(8,128)(2,1)S(1)} %copy.73), channel_id=1, source_target_pairs={{464,0},{480,16},{496,32},{0,48},{16,64},{32,80},{48,96},{64,112},... | collective-permute-start | bytes 3145736 | tf_op jit(solution)/shard_map/ppermute | solution.py:12
  13.1 158.5 %collective-permute-start.2 = (bf16[16,1,2,128,128]{3,4,0,2,1:T(8,128)(2,1)S(1)}, bf16[16,1,2,128,128]{3,4,0,2,1:T(8,128)(2,1)S(1)}, u32[]{:S(2)}, u32[]{:S(2)}) collective-permute-start(bf16[16,1,2,128,128]{3,4,0,2,1:T(8,128)(2,1)S(1)} %copy.73), channel_id=1, source_target_pairs={{480,0},{496,16},{0,32},{16,48},{32,64},{48,80},{64,96},{80,112},{... | collective-permute-start | bytes 3145736 | tf_op jit(solution)/shard_map/ppermute | solution.py:12
  15.1 177.7 %collective-permute-start.3 = (bf16[16,1,2,128,128]{3,4,0,2,1:T(8,128)(2,1)S(1)}, bf16[16,1,2,128,128]{3,4,0,2,1:T(8,128)(2,1)}, u32[]{:S(2)}, u32[]{:S(2)}) collective-permute-start(bf16[16,1,2,128,128]{3,4,0,2,1:T(8,128)(2,1)S(1)} %copy.73), channel_id=1, source_target_pairs={{496,0},{0,16},{16,32},{32,48},{48,64},{64,80},{80,96},{96,112},{1... | collective-permute-start | bytes 3145736 | tf_op jit(solution)/shard_map/ppermute | solution.py:12
  19.4 173.4 %collective-permute-start.4 = (bf16[16,1,2,128,128]{3,4,0,2,1:T(8,128)(2,1)S(1)}, bf16[16,1,2,128,128]{3,4,0,2,1:T(8,128)(2,1)}, u32[]{:S(2)}, u32[]{:S(2)}) collective-permute-start(bf16[16,1,2,128,128]{3,4,0,2,1:T(8,128)(2,1)S(1)} %copy.73), channel_id=1, source_target_pairs={{16,0},{32,16},{48,32},{64,48},{80,64},{96,80},{112,96},{128,112},... | collective-permute-start | bytes 3145736 | tf_op jit(solution)/shard_map/ppermute | solution.py:12
  28.5 176.9 %collective-permute-start.5 = (bf16[16,1,2,128,128]{3,4,0,2,1:T(8,128)(2,1)S(1)}, bf16[16,1,2,128,128]{3,4,0,2,1:T(8,128)(2,1)}, u32[]{:S(2)}, u32[]{:S(2)}) collective-permute-start(bf16[16,1,2,128,128]{3,4,0,2,1:T(8,128)(2,1)S(1)} %copy.73), channel_id=1, source_target_pairs={{32,0},{48,16},{64,32},{80,48},{96,64},{112,80},{128,96},{144,112}... | collective-permute-start | bytes 3145736 | tf_op jit(solution)/shard_map/ppermute | solution.py:12
  120.3 85.0 %collective-permute-start.6 = (bf16[16,1,2,128,128]{3,4,0,2,1:T(8,128)(2,1)S(1)}, bf16[16,1,2,128,128]{3,4,0,2,1:T(8,128)(2,1)}, u32[]{:S(2)}, u32[]{:S(2)}) collective-permute-start(bf16[16,1,2,128,128]{3,4,0,2,1:T(8,128)(2,1)S(1)} %copy.73), channel_id=1, source_target_pairs={{48,0},{64,16},{80,32},{96,48},{112,64},{128,80},{144,96},{160,112... | collective-permute-start | bytes 3145736 | tf_op jit(solution)/shard_map/ppermute | solution.py:12
  171.6 1.0 copy-start.1
  172.6 32.7 %collective-permute-start.7 = (bf16[16,1,2,128,128]{3,4,0,2,1:T(8,128)(2,1)S(1)}, bf16[16,1,2,128,128]{3,4,0,2,1:T(8,128)(2,1)}, u32[]{:S(2)}, u32[]{:S(2)}) collective-permute-start(bf16[16,1,2,128,128]{3,4,0,2,1:T(8,128)(2,1)S(1)} %copy.73), channel_id=1, source_target_pairs={{64,0},{80,16},{96,32},{112,48},{128,64},{144,80},{160,96},{176,11... | collective-permute-start | bytes 3145736 | tf_op jit(solution)/shard_map/ppermute | solution.py:12
  175.3 44.3 %all-to-all-start = ((s32[16,1,2]{2,1,0:T(1,128)}), s32[16,1,2]{2,1,0:T(1,128)S(1)}, u32[]{:S(2)}, u32[]{:S(2)}) async-start(s32[16,1,2]{2,1,0:T(1,128)} %bitcast), calls=%async_computation | async-start | bytes 16384 | tf_op jit(solution)/shard_map/all_to_all | solution.py:94
  205.3 4.5 %copy-start = (bf16[16,3,2,128,128]{4,3,2,1,0:T(8,128)(2,1)S(1)}, bf16[16,3,2,128,128]{4,3,2,1,0:T(8,128)(2,1)}, u32[]{:S(2)}) copy-start(bf16[16,3,2,128,128]{4,3,2,1,0:T(8,128)(2,1)} %param.6) | copy-start | bytes 9437188
  219.6 61.5 %all-to-all-start.1 = ((bf16[16,2,1,2,128,128]{5,4,3,1,2,0:T(8,128)(2,1)}), bf16[16,2,1,2,128,128]{5,4,3,1,2,0:T(8,128)(2,1)S(1)}, u32[]{:S(2)}, u32[]{:S(2)}) async-start(bf16[16,2,1,2,128,128]{5,4,3,1,2,0:T(8,128)(2,1)} %bitcast.47), calls=%async_computation.1 | async-start | bytes 4194304 | tf_op jit(solution)/shard_map/all_to_all | solution.py:93
where the time goes:
time: 288 us
  waiting for transfers between devices  209 us (73%)
  starting transfers between devices  53.1 us (18%)
  local copies, waits for them, and re-layouts  11.6 us (4%)
  matrix products  8.38 us (3%)
  other arithmetic  5.58 us (2%)
    ppermute x8, waiting for transfers between devices, shifted(): return lax.ppermute(block, axis, route)  159 us
    all_to_all x1, waiting for transfers between devices, body(): lax.all_to_all(outgoing, 'atom', split_axis=0, concat_axis=0, tiled=True)  50.1 us
    ppermute x8, starting transfers between devices, shifted(): return lax.ppermute(block, axis, route)  32.8 us
    all_to_all x1, starting transfers between devices, body(): lax.all_to_all(slot_atom, 'atom', split_axis=0, concat_axis=0, tiled=True)  10.2 us
    all_to_all x1, starting transfers between devices, body(): lax.all_to_all(outgoing, 'atom', split_axis=0, concat_axis=0, tiled=True)  10.1 us
    unnamed x13, local copies, waits for them, and re-layouts  6.56 us
  transfers between devices with their start and end apart: 10, of which 6 were waited for; matrix products, arithmetic and copies ran while one was open for 6% of the time, Pallas kernels for 0%

commit v1 on v0

v1 whole, which is shorter than its diff:
```python
import functools

import jax
import jax.numpy as jnp
from jax import lax
from jax.experimental import pallas as pl
from jax.experimental.pallas import tpu as pltpu
from jax.sharding import PartitionSpec as P

MESH = pl.DeviceIdType.MESH
N = 128
BONDS = 16
OWNERS = 16
ATOMS = 8
MODES = 4
PARTS = 4
ROWS = N // PARTS
CHUNKS = 8
NB = BONDS // CHUNKS
STEPS = 4
STRIP = N // STEPS
BF = jnp.bfloat16
F32 = jnp.float32


def kernel(
    green, coupling, weight, offset, bond_atom, out,
    part, low, high, mixed_part, mixed, coup, bond_self,
    pack, arrived, meta, meta_in, own_sum, core_out, core_in, kept, far_out, far_in,
    slot_bond, table,
    in_send, in_recv, row_send, row_recv, back_send, back_recv, own_sem, mix_sem, coup_sem,
    meta_send, meta_recv, x_send, x_recv, core_send, core_recv, far_send, far_recv,
):
    e = lax.axis_index("energy")
    a = lax.axis_index("atom")
    y, zl = lax.div(e, PARTS), lax.rem(e, PARTS)
    x, zh, co = lax.div(a, 4), lax.rem(lax.div(a, 2), 2), lax.rem(a, 2)
    in_row = [(y * PARTS + lax.rem(zl + s, PARTS), a) for s in range(PARTS)]
    up = (lax.rem(y + 1, 8) * PARTS + zl, a)
    down = (lax.rem(y + 7, 8) * PARTS + zl, a)
    in_x = [(e, lax.rem(x + s, 4) * 4 + zh * 2 + co) for s in range(4)]
    other_core = (e, x * 4 + zh * 2 + 1 - co)
    far = (e, x * 4 + (1 - zh) * 2 + co)

    barrier = pltpu.get_barrier_semaphore()
    peers = in_row[1:] + [up, down] + in_x[1:] + [other_core, far]
    for peer in peers:
        pl.semaphore_signal(barrier, inc=1, device_id=peer, device_id_type=MESH)
    load_coup = pltpu.make_async_copy(coupling, coup, coup_sem)
    load_coup.start()
    own_load = pltpu.make_async_copy(
        green.at[:, :, pl.ds(pl.multiple_of(zl * ROWS, ROWS), ROWS), :], part.at[zl], own_sem
    )
    own_load.start()
    pl.semaphore_wait(barrier, len(peers))

    def remote(src, dst, send, recv, device):
        return pltpu.make_async_remote_copy(
            src_ref=src, dst_ref=dst, send_sem=send, recv_sem=recv, device_id=device, device_id_type=MESH
        )

    def bonds_of(q):
        return pl.ds(q * NB, NB)

    def in_copy(q, s):
        other = lax.rem(zl + s, PARTS)
        rows = pl.ds(pl.multiple_of(other * ROWS, ROWS), ROWS)
        return remote(
            green.at[bonds_of(q), :, rows, :], part.at[zl, bonds_of(q)],
            in_send.at[q, s], in_recv.at[q, zl], in_row[s],
        )

    def in_arrival(q, s):
        other = lax.rem(zl + s, PARTS)
        block = part.at[other, bonds_of(q)]
        return remote(block, block, in_send.at[q, s], in_recv.at[q, other], in_row[s])

    def row_copy(q, way):
        src = part.at[:, bonds_of(q)]
        dst = (low if way == 0 else high).at[:, bonds_of(q)]
        return remote(src, dst, row_send.at[q, way], row_recv.at[q, way], up if way == 0 else down)

    own_rows = pl.ds(pl.multiple_of(zl * ROWS, ROWS), ROWS)

    def back_copy(q, s):
        other = lax.rem(zl + s, PARTS)
        return remote(
            mixed_part.at[other, bonds_of(q)], mixed.at[bonds_of(q), :, own_rows, :],
            back_send.at[q, s], back_recv.at[q, zl], in_row[s],
        )

    def back_arrival(q, s):
        other = lax.rem(zl + s, PARTS)
        rows = pl.ds(pl.multiple_of(other * ROWS, ROWS), ROWS)
        block = mixed.at[bonds_of(q), :, rows, :]
        return remote(block, block, back_send.at[q, s], back_recv.at[q, other], in_row[s])

    def own_mixed(q):
        return pltpu.make_async_copy(
            mixed_part.at[zl, bonds_of(q)], mixed.at[bonds_of(q), :, own_rows, :], mix_sem.at[q]
        )

    @pl.loop(0, CHUNKS)
    def _(q):
        for s in (2, 1, 3):
            in_copy(q, s).start()

    @pl.loop(0, BONDS)
    def _(b):
        for d in range(1, MODES + 1):
            below = jnp.float32(0)
            above = jnp.float32(0)
            for mode in range(MODES):
                hit = offset[b, mode] == d
                below = below + jnp.where(hit, weight[0, b, mode], jnp.float32(0))
                above = above + jnp.where(hit, weight[1, b, mode], jnp.float32(0))
            table[b, d - 1] = below
            table[b, MODES + d - 1] = above

    @pl.loop(0, OWNERS)
    def _(owner):
        first = jnp.int32(BONDS)
        last = jnp.int32(-1)
        for b in range(BONDS):
            hit = lax.div(bond_atom[b], ATOMS) == owner
            first = jnp.minimum(first, jnp.where(hit, b, BONDS))
            last = jnp.maximum(last, jnp.where(hit, b, -1))
        named = last >= 0
        for place, bond in enumerate((first, last)):
            bond = jnp.clip(bond, 0, BONDS - 1)
            slot_bond[owner, place] = bond
            atom = jnp.where(named, lax.rem(bond_atom[bond], ATOMS), -1)
            meta[owner, place] = jnp.full((8, N), atom.astype(F32), F32)

    own_load.wait()

    def meta_copy(s):
        other = lax.rem(x + s, 4)
        return remote(meta.at[pl.ds(other * 4, 4)], meta_in.at[x], meta_send.at[s], meta_recv.at[x], in_x[s])

    def meta_arrival(s):
        other = lax.rem(x + s, 4)
        return remote(meta_in.at[other], meta_in.at[other], meta_send.at[s], meta_recv.at[other], in_x[s])

    def forward(q):
        for s in range(1, PARTS):
            in_arrival(q, s).wait_recv()
        row_copy(q, 0).start()
        row_copy(q, 1).start()

    def mix(q):
        row_copy(q, 0).wait_recv()
        row_copy(q, 1).wait_recv()

        @pl.loop(0, NB)
        def _(n):
            b = q * NB + n
            below = [table[b, d] for d in range(MODES)]
            above = [table[b, MODES + d] for d in range(MODES)]
            for half in range(2):
                total = [None] * PARTS

                def add(t, factor, block):
                    term = factor * block
                    total[t] = term if total[t] is None else total[t] + term

                for k in range(PARTS):
                    block = part[k, b, half].astype(F32)
                    for t in range(PARTS):
                        if k < t:
                            add(t, below[t - k - 1], block)
                        if k > t:
                            add(t, above[k - t - 1], block)
                    block = low[k, b, half].astype(F32)
                    for t in range(k + 1):
                        add(t, below[MODES - k + t - 1], block)
                    block = high[k, b, half].astype(F32)
                    for t in range(k, PARTS):
                        add(t, above[MODES + k - t - 1], block)
                for t in range(PARTS):
                    mixed_part[t, b, half] = total[t].astype(BF)

        for s in (2, 1, 3):
            back_copy(q, s).start()
        own_mixed(q).start()

    def multiply(q):
        for s in range(1, PARTS):
            back_arrival(q, s).wait_recv()
        own_mixed(q).wait()

        @pl.loop(0, NB)
        def _(n):
            b = q * NB + n
            f_re, f_im = mixed[b, 0], mixed[b, 1]
            f_all = jnp.concatenate(
                [jnp.concatenate([f_re, f_im], axis=1), jnp.concatenate([-f_im, f_re], axis=1)], axis=0
            )
            acc = jnp.zeros((N, 2 * N), F32)
            for c in range(3):
                h_re, h_im = coup[b, c, 0], coup[b, c, 1]
                h_row = jnp.concatenate([h_re, h_im], axis=1)
                left = jnp.dot(h_row, f_all, preferred_element_type=F32).astype(BF)
                h_all = jnp.concatenate(
                    [jnp.concatenate([h_re, -h_im], axis=1), jnp.concatenate([h_im, h_re], axis=1)], axis=0
                )
                acc = acc + lax.dot_general(
                    left, h_all, (((1,), (1,)), ((), ())), preferred_element_type=F32
                )
            bond_self[b, 0] = acc[:, :N].astype(BF)
            bond_self[b, 1] = acc[:, N:].astype(BF)

    forward(0)
    for s in range(1, 4):
        meta_copy(s).start()
    forward(1)
    mix(0)
    load_coup.wait()

    @pl.loop(2, CHUNKS)
    def _(q):
        forward(q)
        mix(q - 1)
        multiply(q - 2)

    mix(CHUNKS - 1)
    multiply(CHUNKS - 2)
    multiply(CHUNKS - 1)

    def x_copy(r, s):
        other = lax.rem(x + s, 4)
        return remote(
            pack.at[r, pl.ds(other * 4, 4)], arrived.at[r, x], x_send.at[r, s], x_recv.at[r, x], in_x[s]
        )

    def x_arrival(r, s):
        other = lax.rem(x + s, 4)
        block = arrived.at[r, other]
        return remote(block, block, x_send.at[r, s], x_recv.at[r, other], in_x[s])

    def core_copy(r):
        return remote(core_out.at[r], core_in.at[r], core_send.at[r], core_recv.at[r], other_core)

    def far_copy(r):
        return remote(far_out.at[r], far_in.at[r], far_send.at[r], far_recv.at[r], far)

    for r in range(STEPS):
        @pl.loop(0, OWNERS)
        def _(owner):
            for place in range(2):
                bond = slot_bond[owner, place]
                pack[r, owner, place] = bond_self[bond, :, r * STRIP : (r + 1) * STRIP, :]

        for s in (2, 1, 3):
            x_copy(r, s).start()

    for s in range(1, 4):
        meta_arrival(s).wait_recv()

    def gather(r):
        for s in range(1, 4):
            x_arrival(r, s).wait_recv()

        @pl.loop(0, 4)
        def _(turn):
            zd, other = lax.div(turn, 2), lax.rem(turn, 2)
            place_c = lax.rem(co + other, 2)
            at = zd * 2 + place_c
            for half in range(2):
                blocks = []
                names = []
                for s in range(4):
                    src = lax.rem(x + s, 4)
                    for place in range(2):
                        if s == 0:
                            blocks.append(pack[r, x * 4 + at, place, half].astype(F32))
                            names.append(meta[x * 4 + at, place])
                        else:
                            blocks.append(arrived[r, src, at, place, half].astype(F32))
                            names.append(meta_in[src, at, place])
                blocks = [v.reshape(STRIP // 8, 8, N) for v in blocks]
                for atom in range(ATOMS):
                    total = jnp.zeros((STRIP // 8, 8, N), F32)
                    for v, name in zip(blocks, names):
                        total = total + jnp.where((name == atom)[None], v, 0.0)
                    own_sum[other, zd, atom, half] = total.reshape(STRIP, N)

        core_out[r] = own_sum[1].astype(BF)
        kept[r] = own_sum[0]
        core_copy(r).start()

    def cross(r):
        core_copy(r).wait_recv()
        far_out[r] = (kept[r, 1 - zh] + core_in[r, 1 - zh].astype(F32)).astype(BF)
        kept[r, zh] = kept[r, zh] + core_in[r, zh].astype(F32)
        far_copy(r).start()

    def finish(r):
        far_copy(r).wait_recv()
        out[:, :, r * STRIP : (r + 1) * STRIP, :] = (kept[r, zh] + far_in[r].astype(F32)).astype(BF)

    for r in range(STEPS + 2):
        if r < STEPS:
            gather(r)
        if 1 <= r < STEPS + 1:
            cross(r - 1)
        if r >= 2:
            finish(r - 2)

    @pl.loop(0, CHUNKS)
    def _(q):
        for s in range(1, PARTS):
            in_copy(q, s).wait_send()
            back_copy(q, s).wait_send()
        row_copy(q, 0).wait_send()
        row_copy(q, 1).wait_send()

    for s in range(1, 4):
        meta_copy(s).wait_send()
    for r in range(STEPS):
        for s in range(1, 4):
            x_copy(r, s).wait_send()
        core_copy(r).wait_send()
        far_copy(r).wait_send()


def body(green_blocks, coupling, phonon_weight, offsets, bond_atom):
    green = green_blocks.reshape(BONDS, 2, N, N)
    vmem, smem, dma = pltpu.VMEM, pltpu.SMEM, pltpu.SemaphoreType.DMA
    any_space = pl.BlockSpec(memory_space=pl.ANY)
    small = pl.BlockSpec(memory_space=pltpu.SMEM)
    part = vmem((PARTS, BONDS, 2, ROWS, N), BF)
    out = pl.pallas_call(
        kernel,
        out_shape=jax.ShapeDtypeStruct((ATOMS, 2, N, N), BF),
        in_specs=[any_space, any_space, small, small, small],
        out_specs=pl.BlockSpec(memory_space=pltpu.VMEM),
        scratch_shapes=[
            part, part, part, part,
            vmem((BONDS, 2, N, N), BF),
            vmem((BONDS, 3, 2, N, N), BF),
            vmem((BONDS, 2, N, N), BF),
            vmem((STEPS, OWNERS, 2, 2, STRIP, N), BF),
            vmem((STEPS, 4, 4, 2, 2, STRIP, N), BF),
            vmem((OWNERS, 2, 8, N), F32),
            vmem((4, 4, 2, 8, N), F32),
            vmem((2, 2, ATOMS, 2, STRIP, N), F32),
            vmem((STEPS, 2, ATOMS, 2, STRIP, N), BF),
            vmem((STEPS, 2, ATOMS, 2, STRIP, N), BF),
            vmem((STEPS, 2, ATOMS, 2, STRIP, N), F32),
            vmem((STEPS, ATOMS, 2, STRIP, N), BF),
            vmem((STEPS, ATOMS, 2, STRIP, N), BF),
            smem((OWNERS, 2), jnp.int32),
            smem((BONDS, 2 * MODES), F32),
            dma((CHUNKS, PARTS)), dma((CHUNKS, PARTS)),
            dma((CHUNKS, 2)), dma((CHUNKS, 2)),
            dma((CHUNKS, PARTS)), dma((CHUNKS, PARTS)),
            dma, dma((CHUNKS,)), dma,
            dma((4,)), dma((4,)),
            dma((STEPS, 4)), dma((STEPS, 4)),
            dma((STEPS,)), dma((STEPS,)),
            dma((STEPS,)), dma((STEPS,)),
        ],
        compiler_params=pltpu.CompilerParams(
            collective_id=0, has_side_effects=True, vmem_limit_bytes=48 * 1024 * 1024
        ),
    )(green, coupling, phonon_weight, offsets, bond_atom)
    return out.reshape(ATOMS, 1, 2, N, N)


def solution(mesh):
    placed = (
        P("atom", "energy", None, None, None),
        P("atom", None, None, None, None),
        P(None, "atom", None),
        P("atom", None),
        P("atom"),
    )
    return jax.shard_map(
        body,
        mesh=mesh,
        in_specs=placed,
        out_specs=P("atom", "energy", None, None, None),
        check_vma=False,
    )
```

time: 288 us -> 116 us (0.40)
  the two profiles are of different devices: /device:TPU:16 before, /device:TPU:4 now
where the time goes in v1:
time: 116 us; the launch traced here: 115 us
  Pallas kernels  109 us (94%)
  local copies, waits for them, and re-layouts  6.09 us (5%)
    pallas_call x1, Pallas kernels, body(): pl.pallas_call(kernel, out_shape=jax.ShapeDtypeStruct((ATOMS, 2, N, N), B...  109 us
    unnamed x9, local copies, waits for them, and re-layouts  6.09 us

profile of v1, /device:TPU:4, one launch (start us, length us, event | category | flops | bytes accessed | tf_op | source)
XLA Modules:
  0.0 115.3 jit_solution(7559434517682118312)
XLA Ops:
  0.0 0.8 copy.7.offset
  0.8 0.8 copy.6.weight
  1.5 0.0 copy-start
  1.5 1.9 %copy-done = bf16[16,3,2,128,128]{4,3,2,1,0:T(8,128)(2,1)S(1)} copy-done((bf16[16,3,2,128,128]{4,3,2,1,0:T(8,128)(2,1)S(1)}, bf16[16,3,2,128,128]{4,3,2,1,0:T(8,128)(2,1)}, u32[]{:S(2)}) %copy-start) | copy-done | bytes 3145752
  3.4 0.0 copy-start.1
  3.4 1.2 %copy-done.1 = bf16[16,1,2,128,128]{4,3,2,1,0:T(8,128)(2,1)S(1)} copy-done((bf16[16,1,2,128,128]{4,3,2,1,0:T(8,128)(2,1)S(1)}, bf16[16,1,2,128,128]{4,3,2,1,0:T(8,128)(2,1)}, u32[]{:S(2)}) %copy-start.1) | copy-done | bytes 1048600
  4.6 0.0 copy-start.2
  4.6 0.7 copy-done.2
  5.3 109.2 %shard_map.55 = bf16[8,2,128,128]{3,2,1,0:T(8,128)(2,1)S(1)} custom-call(bf16[16,2,128,128]{3,2,1,0:T(8,128)(2,1)S(1)} %bitcast.5, bf16[16,3,2,128,128]{4,3,2,1,0:T(8,128)(2,1)S(1)} %copy-done, f32[2,16,4]{2,1,0:T(8,128)S(1)} %copy.6.weight, s32[16,4]{1,0:T(8,128)S(1)} %copy.7.offset, s32[16]{0:T(128)S(1)} %copy-done.2), custom_call_target="tpu_custom_call" | custom-call | tf_op jit(solution)/shard_map/pallas_call | solution.py:333
  114.5 0.8 copy.10
Async XLA Ops:
  1.5 1.9 %copy-start = (bf16[16,3,2,128,128]{4,3,2,1,0:T(8,128)(2,1)S(1)}, bf16[16,3,2,128,128]{4,3,2,1,0:T(8,128)(2,1)}, u32[]{:S(2)}) copy-start(bf16[16,3,2,128,128]{4,3,2,1,0:T(8,128)(2,1)} %coupling.1) | copy-start | bytes 9437188
  3.4 1.2 %copy-start.1 = (bf16[16,1,2,128,128]{4,3,2,1,0:T(8,128)(2,1)S(1)}, bf16[16,1,2,128,128]{4,3,2,1,0:T(8,128)(2,1)}, u32[]{:S(2)}) copy-start(bf16[16,1,2,128,128]{4,3,2,1,0:T(8,128)(2,1)} %param.5) | copy-start | bytes 3145732
  4.6 0.7 copy-start.2

commit v2 on v1

v2 whole, which is shorter than its diff:
```python
import functools

import jax
import jax.numpy as jnp
from jax import lax
from jax.experimental import pallas as pl
from jax.experimental.pallas import tpu as pltpu
from jax.sharding import PartitionSpec as P

MESH = pl.DeviceIdType.MESH
N = 128
BONDS = 16
OWNERS = 16
ATOMS = 8
MODES = 4
PARTS = 4
ROWS = N // PARTS
CHUNKS = 8
NB = BONDS // CHUNKS
WINDOW = 3
PAIRS = BONDS // 2
BACK_WINDOW = 3
ORDER = (2, 1, 3)
KEYS = (2, 1, 3, 0)
STEPS = 4
STRIP = N // STEPS
BF = jnp.bfloat16
F32 = jnp.float32


def kernel(
    green, coupling, weight_in, offset_in, bond_atom_in, out,
    part, low, high, mixed_part, mixed, coup, bond_self,
    pack, arrived, meta, meta_in, core_out, core_in, kept, far_out, far_in, out_strip,
    weight, offset, bond_atom, first_of, last_of, named_at, pair_of, bond_at, table,
    small_sem, in_send, in_recv, row_send, row_recv, back_send, back_recv, own_sem, mix_sem, coup_sem,
    meta_send, meta_recv, x_send, x_recv, core_send, core_recv, far_send, far_recv, out_sem,
):
    e = lax.axis_index("energy")
    a = lax.axis_index("atom")
    y, zl = lax.div(e, PARTS), lax.rem(e, PARTS)
    x, zh, co = lax.div(a, 4), lax.rem(lax.div(a, 2), 2), lax.rem(a, 2)
    in_row = [(y * PARTS + lax.rem(zl + s, PARTS), a) for s in range(PARTS)]
    up = (lax.rem(y + 1, 8) * PARTS + zl, a)
    down = (lax.rem(y + 7, 8) * PARTS + zl, a)
    in_x = [(e, lax.rem(x + s, 4) * 4 + zh * 2 + co) for s in range(4)]
    other_core = (e, x * 4 + zh * 2 + 1 - co)
    far = (e, x * 4 + (1 - zh) * 2 + co)

    barrier = pltpu.get_barrier_semaphore()
    peers = in_row[1:] + [up, down] + in_x[1:] + [other_core, far]
    for peer in peers:
        pl.semaphore_signal(barrier, inc=1, device_id=peer, device_id_type=MESH)
    small = [
        pltpu.make_async_copy(src, dst, small_sem.at[i])
        for i, (src, dst) in enumerate(
            ((weight_in, weight), (offset_in, offset), (bond_atom_in, bond_atom))
        )
    ]
    for load in small:
        load.start()
    own_rows = pl.ds(pl.multiple_of(zl * ROWS, ROWS), ROWS)
    own_load = pltpu.make_async_copy(green.at[:, :, own_rows, :], part.at[zl], own_sem)
    own_load.start()
    load_coup = pltpu.make_async_copy(coupling, coup, coup_sem)
    load_coup.start()
    pl.semaphore_wait(barrier, len(peers))

    def remote(src, dst, send, recv, device):
        return pltpu.make_async_remote_copy(
            src_ref=src, dst_ref=dst, send_sem=send, recv_sem=recv, device_id=device, device_id_type=MESH
        )

    def rows_of(other):
        return pl.ds(pl.multiple_of(other * ROWS, ROWS), ROWS)

    def in_copy(q, s):
        bonds = pl.ds(q * NB, NB)
        return remote(
            green.at[bonds, :, rows_of(lax.rem(zl + s, PARTS)), :], part.at[zl, bonds],
            in_send.at[q, s], in_recv.at[q, zl], in_row[s],
        )

    def in_arrival(q, s):
        other = lax.rem(zl + s, PARTS)
        block = part.at[other, pl.ds(q * NB, NB)]
        return remote(block, block, in_send.at[q, s], in_recv.at[q, other], in_row[s])

    def row_copy(q, way):
        bonds = pl.ds(q * NB, NB)
        dst = (low if way == 0 else high).at[:, bonds]
        return remote(part.at[:, bonds], dst, row_send.at[q, way], row_recv.at[q, way], up if way == 0 else down)

    def back_copy(p, s):
        two = pl.ds(2 * p, 2)
        return remote(
            mixed_part.at[lax.rem(zl + s, PARTS), two], mixed.at[two, :, own_rows, :],
            back_send.at[p, s], back_recv.at[p, zl], in_row[s],
        )

    def back_arrival(p, s):
        other = lax.rem(zl + s, PARTS)
        block = mixed.at[pl.ds(2 * p, 2), :, rows_of(other), :]
        return remote(block, block, back_send.at[p, s], back_recv.at[p, other], in_row[s])

    def own_mixed(p):
        two = pl.ds(2 * p, 2)
        return pltpu.make_async_copy(mixed_part.at[zl, two], mixed.at[two, :, own_rows, :], mix_sem.at[p])

    def meta_copy(s):
        return remote(meta.at[s], meta_in.at[x], meta_send.at[s], meta_recv.at[x], in_x[s])

    def meta_arrival(s):
        block = meta_in.at[lax.rem(x + s, 4)]
        return remote(block, block, meta_send.at[s], meta_recv.at[lax.rem(x + s, 4)], in_x[s])

    def x_copy(late, kind, s):
        return remote(
            pack.at[late, kind, s], arrived.at[late, kind, x],
            x_send.at[late, kind, s], x_recv.at[late, kind, x], in_x[s],
        )

    def x_arrival(late, kind, s):
        other = lax.rem(x + s, 4)
        block = arrived.at[late, kind, other]
        return remote(block, block, x_send.at[late, kind, s], x_recv.at[late, kind, other], in_x[s])

    def core_copy(late):
        return remote(core_out.at[late], core_in.at[late], core_send.at[late], core_recv.at[late], other_core)

    def far_copy(r):
        return remote(far_out.at[r], far_in.at[r], far_send.at[r], far_recv.at[r], far)

    for q in range(WINDOW):
        for s in ORDER:
            in_copy(q, s).start()
    for load in small:
        load.wait()

    for late in range(2):
        zd = zh if late else 1 - zh
        for kind in range(2):
            for place, s in enumerate(KEYS):
                key = late * 8 + kind * 4 + place
                owner = lax.rem(x + s, 4) * 4 + zd * 2 + (co if kind else 1 - co)
                first = jnp.int32(BONDS)
                last = jnp.int32(-1)
                for b in range(BONDS):
                    hit = lax.div(bond_atom[b], ATOMS) == owner
                    first = jnp.minimum(first, jnp.where(hit, b, BONDS))
                    last = jnp.maximum(last, jnp.where(hit, b, -1))
                named = last >= 0
                first_of[key] = jnp.minimum(first, BONDS - 1)
                last_of[key] = jnp.maximum(last, 0)
                named_at[key] = jnp.where(named, 1, 0)
                for slot, bond in enumerate((first_of[key], last_of[key])):
                    atom = jnp.where(named, lax.rem(bond_atom[bond], ATOMS), -1)
                    meta[s, late, kind, slot] = jnp.full((8, N), atom.astype(F32), F32)

    def count(key, before):
        pair_of[key] = jnp.minimum(before, PAIRS - 1)
        named_at[key] = jnp.where(named_at[key] == 1, before, -1)
        return jnp.where(named_at[key] >= 0, before + 1, before)

    lax.fori_loop(0, OWNERS, count, jnp.int32(0))

    @pl.loop(0, PAIRS)
    def _(p):
        first = jnp.int32(0)
        last = jnp.int32(0)
        for key in range(OWNERS):
            hit = named_at[key] == p
            first = first + jnp.where(hit, first_of[key], 0)
            last = last + jnp.where(hit, last_of[key], 0)
        bond_at[2 * p] = first
        bond_at[2 * p + 1] = last

    @pl.loop(0, BONDS)
    def _(at):
        b = bond_at[at]
        for d in range(1, MODES + 1):
            below = jnp.float32(0)
            above = jnp.float32(0)
            for mode in range(MODES):
                hit = offset[mode, b] == d
                below = below + jnp.where(hit, weight[0, mode, b], jnp.float32(0))
                above = above + jnp.where(hit, weight[1, mode, b], jnp.float32(0))
            table[at, d - 1] = below
            table[at, MODES + d - 1] = above

    own_load.wait()

    @pl.loop(0, CHUNKS - WINDOW)
    def _(q):
        for s in range(1, PARTS):
            in_arrival(q, s).wait_recv()
        for s in ORDER:
            in_copy(q + WINDOW, s).start()
        row_copy(q, 0).start()
        row_copy(q, 1).start()

    for s in range(1, 4):
        meta_copy(s).start()

    @pl.loop(CHUNKS - WINDOW, CHUNKS)
    def _(q):
        for s in range(1, PARTS):
            in_arrival(q, s).wait_recv()
        row_copy(q, 0).start()
        row_copy(q, 1).start()

    load_coup.wait()

    @pl.loop(0, CHUNKS)
    def _(q):
        row_copy(q, 0).wait_recv()
        row_copy(q, 1).wait_recv()

    def mix(p):
        @pl.loop(0, 2)
        def _(n):
            at = 2 * p + n
            b = bond_at[at]
            below = [table[at, d] for d in range(MODES)]
            above = [table[at, MODES + d] for d in range(MODES)]
            for half in range(2):
                total = [None] * PARTS

                def add(t, factor, block):
                    term = factor * block
                    total[t] = term if total[t] is None else total[t] + term

                for k in range(PARTS):
                    block = part[k, b, half].astype(F32)
                    for t in range(PARTS):
                        if k < t:
                            add(t, below[t - k - 1], block)
                        if k > t:
                            add(t, above[k - t - 1], block)
                    block = low[k, b, half].astype(F32)
                    for t in range(k + 1):
                        add(t, below[MODES - k + t - 1], block)
                    block = high[k, b, half].astype(F32)
                    for t in range(k, PARTS):
                        add(t, above[MODES + k - t - 1], block)
                for t in range(PARTS):
                    mixed_part[t, at, half] = total[t].astype(BF)

    def send_back(p):
        for s in ORDER:
            back_copy(p, s).start()
        own_mixed(p).start()

    def multiply(p):
        for s in range(1, PARTS):
            back_arrival(p, s).wait_recv()
        own_mixed(p).wait()
        if p + BACK_WINDOW < PAIRS:
            send_back(p + BACK_WINDOW)

        @pl.loop(0, 2)
        def _(n):
            at = 2 * p + n
            b = bond_at[at]
            f_re, f_im = mixed[at, 0], mixed[at, 1]
            f_all = jnp.concatenate(
                [jnp.concatenate([f_re, f_im], axis=1), jnp.concatenate([-f_im, f_re], axis=1)], axis=0
            )
            acc = jnp.zeros((N, 2 * N), F32)
            for c in range(3):
                h_re, h_im = coup[b, c, 0], coup[b, c, 1]
                h_row = jnp.concatenate([h_re, h_im], axis=1)
                left = jnp.dot(h_row, f_all, preferred_element_type=F32).astype(BF)
                h_all = jnp.concatenate(
                    [jnp.concatenate([h_re, -h_im], axis=1), jnp.concatenate([h_im, h_re], axis=1)], axis=0
                )
                acc = acc + lax.dot_general(
                    left, h_all, (((1,), (1,)), ((), ())), preferred_element_type=F32
                )
            bond_self[at, 0] = acc[:, :N].astype(BF)
            bond_self[at, 1] = acc[:, N:].astype(BF)

    def send_key(key):
        late, kind, s = key // 8, key % 8 // 4, KEYS[key % 4]
        if s == 0:
            return
        pair = pair_of[key]
        for slot in range(2):
            pack[late, kind, s, slot] = bond_self[2 * pair + slot]
        x_copy(late, kind, s).start()

    def gather(late, kind, r, emit):
        rows = pl.ds(pl.multiple_of(r * STRIP, STRIP), STRIP)
        own = 2 * pair_of[late * 8 + kind * 4 + 3]
        for half in range(2):
            blocks = []
            names = []
            for s in range(4):
                src = lax.rem(x + s, 4)
                for slot in range(2):
                    if s == 0:
                        block = bond_self[own + slot, half, rows]
                        names.append(meta[0, late, kind, slot])
                    else:
                        block = arrived[late, kind, src, slot, half, rows]
                        names.append(meta_in[src, late, kind, slot])
                    blocks.append(block.astype(F32).reshape(STRIP // 8, 8, N))
            for atom in range(ATOMS):
                total = jnp.zeros((STRIP // 8, 8, N), F32)
                for block, name in zip(blocks, names):
                    total = total + jnp.where((name == atom)[None], block, 0.0)
                emit(atom, half, rows, total.reshape(STRIP, N))

    def gather_for_core(late):
        for s in range(1, 4):
            x_arrival(late, 0, s).wait_recv()

        @pl.loop(0, STEPS)
        def _(r):
            def emit(atom, half, rows, total):
                core_out[late, atom, half, rows] = total.astype(BF)

            gather(late, 0, r, emit)

        core_copy(late).start()

    for p in range(BACK_WINDOW):
        mix(p)
        send_back(p)
    for p in range(BACK_WINDOW, PAIRS):
        mix(p)
    for p in range(PAIRS):
        multiply(p)
        send_key(p)
        if p == PAIRS - 2:
            for s in range(1, 4):
                meta_arrival(s).wait_recv()
            gather_for_core(0)
    for key in range(8, 16):
        send_key(key)

    for s in range(1, 4):
        x_arrival(0, 1, s).wait_recv()
    core_copy(0).wait_recv()

    @pl.loop(0, STEPS)
    def _(r):
        def emit(atom, half, rows, total):
            far_out[r, atom, half] = (total + core_in[0, atom, half, rows].astype(F32)).astype(BF)

        gather(0, 1, r, emit)
        far_copy(r).start()

    gather_for_core(1)
    for s in range(1, 4):
        x_arrival(1, 1, s).wait_recv()
    core_copy(1).wait_recv()

    @pl.loop(0, STEPS)
    def _(r):
        def emit(atom, half, rows, total):
            kept[r, atom, half] = total + core_in[1, atom, half, rows].astype(F32)

        gather(1, 1, r, emit)

    def out_copy(r):
        rows = pl.ds(pl.multiple_of(r * STRIP, STRIP), STRIP)
        return pltpu.make_async_copy(out_strip.at[r], out.at[:, :, rows, :], out_sem.at[r])

    @pl.loop(0, STEPS)
    def _(r):
        far_copy(r).wait_recv()
        out_strip[r] = (kept[r] + far_in[r].astype(F32)).astype(BF)
        out_copy(r).start()

    @pl.loop(0, CHUNKS)
    def _(q):
        for s in range(1, PARTS):
            in_copy(q, s).wait_send()
        row_copy(q, 0).wait_send()
        row_copy(q, 1).wait_send()

    @pl.loop(0, PAIRS)
    def _(p):
        for s in range(1, PARTS):
            back_copy(p, s).wait_send()

    for s in range(1, 4):
        meta_copy(s).wait_send()
        for late in range(2):
            for kind in range(2):
                x_copy(late, kind, s).wait_send()
    for late in range(2):
        core_copy(late).wait_send()
    for r in range(STEPS):
        far_copy(r).wait_send()
        out_copy(r).wait()


def body(green_blocks, coupling, phonon_weight, offsets, bond_atom):
    green = green_blocks.reshape(BONDS, 2, N, N)
    vmem, smem, dma = pltpu.VMEM, pltpu.SMEM, pltpu.SemaphoreType.DMA
    any_space = pl.BlockSpec(memory_space=pl.ANY)
    part = vmem((PARTS, BONDS, 2, ROWS, N), BF)
    out = pl.pallas_call(
        kernel,
        out_shape=jax.ShapeDtypeStruct((ATOMS, 2, N, N), BF),
        in_specs=[any_space] * 5,
        out_specs=any_space,
        scratch_shapes=[
            part, part, part, part,
            vmem((BONDS, 2, N, N), BF),
            vmem((BONDS, 3, 2, N, N), BF),
            vmem((BONDS, 2, N, N), BF),
            vmem((2, 2, 4, 2, 2, N, N), BF),
            vmem((2, 2, 4, 2, 2, N, N), BF),
            vmem((4, 2, 2, 2, 8, N), F32),
            vmem((4, 2, 2, 2, 8, N), F32),
            vmem((2, ATOMS, 2, N, N), BF),
            vmem((2, ATOMS, 2, N, N), BF),
            vmem((STEPS, ATOMS, 2, STRIP, N), F32),
            vmem((STEPS, ATOMS, 2, STRIP, N), BF),
            vmem((STEPS, ATOMS, 2, STRIP, N), BF),
            vmem((STEPS, ATOMS, 2, STRIP, N), BF),
            smem((2, MODES, BONDS), F32), smem((MODES, BONDS), jnp.int32), smem((BONDS,), jnp.int32),
            smem((OWNERS,), jnp.int32), smem((OWNERS,), jnp.int32), smem((OWNERS,), jnp.int32),
            smem((OWNERS,), jnp.int32), smem((BONDS,), jnp.int32), smem((BONDS, 2 * MODES), F32),
            dma((3,)), dma((CHUNKS, PARTS)), dma((CHUNKS, PARTS)),
            dma((CHUNKS, 2)), dma((CHUNKS, 2)),
            dma((PAIRS, PARTS)), dma((PAIRS, PARTS)),
            dma, dma((PAIRS,)), dma,
            dma((4,)), dma((4,)),
            dma((2, 2, 4)), dma((2, 2, 4)),
            dma((2,)), dma((2,)),
            dma((STEPS,)), dma((STEPS,)), dma((STEPS,)),
        ],
        compiler_params=pltpu.CompilerParams(
            collective_id=0, has_side_effects=True, vmem_limit_bytes=63 * 1024 * 1024
        ),
    )(green, coupling, phonon_weight.transpose(0, 2, 1), offsets.T, bond_atom)
    return out.reshape(ATOMS, 1, 2, N, N)


def solution(mesh):
    placed = (
        P("atom", "energy", None, None, None),
        P("atom", None, None, None, None),
        P(None, "atom", None),
        P("atom", None),
        P("atom"),
    )
    return jax.shard_map(
        body,
        mesh=mesh,
        in_specs=placed,
        out_specs=P("atom", "energy", None, None, None),
        check_vma=False,
    )
```

time: 116 us -> 99.8 us (0.86)
  the two profiles are of different devices: /device:TPU:4 before, /device:TPU:66 now
where the time goes in v2:
time: 99.8 us; the launch traced here: 99.4 us
  Pallas kernels  97.5 us (98%)
  local copies, waits for them, and re-layouts  1.89 us (2%)
    pallas_call x1, Pallas kernels, body(): pl.pallas_call(kernel, out_shape=jax.ShapeDtypeStruct((ATOMS, 2, N, N), B...  97.5 us

profile of v2, /device:TPU:66, one launch (start us, length us, event | category | flops | bytes accessed | tf_op | source)
XLA Modules:
  0.0 99.4 jit_solution(9341025136904367643)
XLA Ops:
  0.0 97.5 %shard_map.55 = bf16[8,2,128,128]{3,2,1,0:T(8,128)(2,1)} custom-call(bf16[16,2,128,128]{3,2,1,0:T(8,128)(2,1)} %bitcast.7, bf16[16,3,2,128,128]{4,3,2,1,0:T(8,128)(2,1)} %coupling.1, f32[2,4,16]{2,1,0:T(4,128)} %bitcast.8, s32[4,16]{1,0:T(4,128)} %bitcast.9, s32[16]{0:T(128)} %bond_atom_in.1), custom_call_target="tpu_custom_call" | custom-call | tf_op jit(solution)/shard_map/pallas_call | solution.py:405
  97.6 1.9 %copy.8 = bf16[8,1,2,128,128]{4,3,2,1,0:T(8,128)(2,1)} copy(bf16[8,1,2,128,128]{4,3,2,1,0:T(8,128)(2,1)} %bitcast.6) | data formatting | bytes 1048576

commit v3 on v2

--- a/solution.py
+++ b/solution.py
@@ -17,22 +17,27 @@
 ROWS = N // PARTS
 CHUNKS = 8
 NB = BONDS // CHUNKS
-WINDOW = 3
+WINDOW = 2
 PAIRS = BONDS // 2
 BACK_WINDOW = 3
+EARLY = 2
 ORDER = (2, 1, 3)
-KEYS = (2, 1, 3, 0)
+KEYS = (2, 1, 3)
 STEPS = 4
 STRIP = N // STEPS
 BF = jnp.bfloat16
 F32 = jnp.float32
 
 
+def key_index(late, kind, s):
+    return late * 8 + (kind * 3 + KEYS.index(s) if s else 6 + kind)
+
+
 def kernel(
     green, coupling, weight_in, offset_in, bond_atom_in, out,
     part, low, high, mixed_part, mixed, coup, bond_self,
     pack, arrived, meta, meta_in, core_out, core_in, kept, far_out, far_in, out_strip,
-    weight, offset, bond_atom, first_of, last_of, named_at, pair_of, bond_at, table,
+    weight, offset, bond_atom, key_of, place_of, bond_at, slot_at, table,
     small_sem, in_send, in_recv, row_send, row_recv, back_send, back_recv, own_sem, mix_sem, coup_sem,
     meta_send, meta_recv, x_send, x_recv, core_send, core_recv, far_send, far_recv, out_sem,
 ):
@@ -125,8 +130,10 @@
         block = arrived.at[late, kind, other]
         return remote(block, block, x_send.at[late, kind, s], x_recv.at[late, kind, other], in_x[s])
 
-    def core_copy(late):
-        return remote(core_out.at[late], core_in.at[late], core_send.at[late], core_recv.at[late], other_core)
+    def core_copy(late, r):
+        return remote(
+            core_out.at[late, r], core_in.at[late, r], core_send.at[late, r], core_recv.at[late, r], other_core
+        )
 
     def far_copy(r):
         return remote(far_out.at[r], far_in.at[r], far_send.at[r], far_recv.at[r], far)
@@ -137,43 +144,47 @@
     for load in small:
         load.wait()
 
+    @pl.loop(0, BONDS)
+    def _(b):
+        owner = lax.div(bond_atom[b], ATOMS)
+        turn = lax.rem(lax.div(owner, 4) + 4 - x, 4)
+        place = jnp.where(turn == 2, 0, jnp.where(turn == 1, 1, 2))
+        late = jnp.where(lax.rem(lax.div(owner, 2), 2) == zh, 8, 0)
+        kind = jnp.where(lax.rem(owner, 2) == co, 1, 0)
+        key_of[b] = late + jnp.where(turn == 0, 6 + kind, 3 * kind + place)
+        place_of[b] = b
+
+    @pl.loop(EARLY, BONDS)
+    def _(b):
+        mine = key_of[b] * BONDS + b
+        rank = jnp.int32(EARLY)
+        for other in range(EARLY, BONDS):
+            rank = rank + jnp.where(key_of[other] * BONDS + other < mine, 1, 0)
+        place_of[b] = rank
+
+    @pl.loop(0, BONDS)
+    def _(at):
+        found = jnp.int32(0)
+        for b in range(BONDS):
+            found = found + jnp.where(place_of[b] == at, b, 0)
+        bond_at[at] = found
+
     for late in range(2):
-        zd = zh if late else 1 - zh
         for kind in range(2):
-            for place, s in enumerate(KEYS):
-                key = late * 8 + kind * 4 + place
-                owner = lax.rem(x + s, 4) * 4 + zd * 2 + (co if kind else 1 - co)
+            for s in range(4):
+                key = key_index(late, kind, s)
                 first = jnp.int32(BONDS)
                 last = jnp.int32(-1)
                 for b in range(BONDS):
-                    hit = lax.div(bond_atom[b], ATOMS) == owner
+                    hit = key_of[b] == key
                     first = jnp.minimum(first, jnp.where(hit, b, BONDS))
                     last = jnp.maximum(last, jnp.where(hit, b, -1))
                 named = last >= 0
-                first_of[key] = jnp.minimum(first, BONDS - 1)
-                last_of[key] = jnp.maximum(last, 0)
-                named_at[key] = jnp.where(named, 1, 0)
-                for slot, bond in enumerate((first_of[key], last_of[key])):
+                for slot, bond in enumerate((first, last)):
+                    bond = jnp.minimum(jnp.maximum(bond, 0), BONDS - 1)
+                    slot_at[key, slot] = jnp.where(named, place_of[bond], 0)
                     atom = jnp.where(named, lax.rem(bond_atom[bond], ATOMS), -1)
                     meta[s, late, kind, slot] = jnp.full((8, N), atom.astype(F32), F32)
-
-    def count(key, before):
-        pair_of[key] = jnp.minimum(before, PAIRS - 1)
-        named_at[key] = jnp.where(named_at[key] == 1, before, -1)
-        return jnp.where(named_at[key] >= 0, before + 1, before)
-
-    lax.fori_loop(0, OWNERS, count, jnp.int32(0))
-
-    @pl.loop(0, PAIRS)
-    def _(p):
-        first = jnp.int32(0)
-        last = jnp.int32(0)
-        for key in range(OWNERS):
-            hit = named_at[key] == p
-            first = first + jnp.where(hit, first_of[key], 0)
-            last = last + jnp.where(hit, last_of[key], 0)
-        bond_at[2 * p] = first
-        bond_at[2 * p + 1] = last
 
     @pl.loop(0, BONDS)
     def _(at):
@@ -209,18 +220,11 @@
         row_copy(q, 0).start()
         row_copy(q, 1).start()
 
-    load_coup.wait()
-
-    @pl.loop(0, CHUNKS)
-    def _(q):
-        row_copy(q, 0).wait_recv()
-        row_copy(q, 1).wait_recv()
-
     def mix(p):
         @pl.loop(0, 2)
         def _(n):
             at = 2 * p + n
-            b = bond_at[at]
+            b = at if p < EARLY // 2 else bond_at[at]
             below = [table[at, d] for d in range(MODES)]
             above = [table[at, MODES + d] for d in range(MODES)]
             for half in range(2):
@@ -280,18 +284,15 @@
             bond_self[at, 0] = acc[:, :N].astype(BF)
             bond_self[at, 1] = acc[:, N:].astype(BF)
 
-    def send_key(key):
-        late, kind, s = key // 8, key % 8 // 4, KEYS[key % 4]
-        if s == 0:
-            return
-        pair = pair_of[key]
+    def send_key(late, kind, s):
+        key = key_index(late, kind, s)
         for slot in range(2):
-            pack[late, kind, s, slot] = bond_self[2 * pair + slot]
+            pack[late, kind, s, slot] = bond_self[slot_at[key, slot]]
         x_copy(late, kind, s).start()
 
     def gather(late, kind, r, emit):
         rows = pl.ds(pl.multiple_of(r * STRIP, STRIP), STRIP)
-        own = 2 * pair_of[late * 8 + kind * 4 + 3]
+        own = key_index(late, kind, 0)
         for half in range(2):
             blocks = []
             names = []
@@ -299,7 +300,7 @@
                 src = lax.rem(x + s, 4)
                 for slot in range(2):
                     if s == 0:
-                        block = bond_self[own + slot, half, rows]
+                        block = bond_self[slot_at[own, slot], half, rows]
                         names.append(meta[0, late, kind, slot])
                     else:
                         block = arrived[late, kind, src, slot, half, rows]
@@ -318,49 +319,65 @@
         @pl.loop(0, STEPS)
         def _(r):
             def emit(atom, half, rows, total):
-                core_out[late, atom, half, rows] = total.astype(BF)
+                core_out[late, r, atom, half] = total.astype(BF)
 
             gather(late, 0, r, emit)
-
-        core_copy(late).start()
-
-    for p in range(BACK_WINDOW):
+            core_copy(late, r).start()
+
+    def rows_arrived(q):
+        row_copy(q, 0).wait_recv()
+        row_copy(q, 1).wait_recv()
+
+    for q in range(EARLY // NB):
+        rows_arrived(q)
+    for p in range(EARLY // 2):
+        mix(p)
+        send_back(p)
+    load_coup.wait()
+
+    @pl.loop(EARLY // NB, CHUNKS)
+    def _(q):
+        rows_arrived(q)
+
+    for p in range(EARLY // 2, BACK_WINDOW):
         mix(p)
         send_back(p)
     for p in range(BACK_WINDOW, PAIRS):
         mix(p)
     for p in range(PAIRS):
         multiply(p)
-        send_key(p)
-        if p == PAIRS - 2:
-            for s in range(1, 4):
-                meta_arrival(s).wait_recv()
-            gather_for_core(0)
-    for key in range(8, 16):
-        send_key(key)
-
+        for kind in range(2):
+            for s in KEYS:
+                if p == min(key_index(0, kind, s) + EARLY // 2, PAIRS - 1):
+                    send_key(0, kind, s)
+    for s in range(1, 4):
+        meta_arrival(s).wait_recv()
+    gather_for_core(0)
     for s in range(1, 4):
         x_arrival(0, 1, s).wait_recv()
-    core_copy(0).wait_recv()
 
     @pl.loop(0, STEPS)
     def _(r):
         def emit(atom, half, rows, total):
-            far_out[r, atom, half] = (total + core_in[0, atom, half, rows].astype(F32)).astype(BF)
-
+            far_out[r, atom, half] = (total + core_in[0, r, atom, half].astype(F32)).astype(BF)
+
+        core_copy(0, r).wait_recv()
         gather(0, 1, r, emit)
         far_copy(r).start()
 
+    for kind in range(2):
+        for s in KEYS:
+            send_key(1, kind, s)
     gather_for_core(1)
     for s in range(1, 4):
         x_arrival(1, 1, s).wait_recv()
-    core_copy(1).wait_recv()
 
     @pl.loop(0, STEPS)
     def _(r):
         def emit(atom, half, rows, total):
-            kept[r, atom, half] = total + core_in[1, atom, half, rows].astype(F32)
-
+            kept[r, atom, half] = total + core_in[1, r, atom, half].astype(F32)
+
+        core_copy(1, r).wait_recv()
         gather(1, 1, r, emit)
 
     def out_copy(r):
@@ -390,9 +407,9 @@
         for late in range(2):
             for kind in range(2):
                 x_copy(late, kind, s).wait_send()
-    for late in range(2):
-        core_copy(late).wait_send()
     for r in range(STEPS):
+        for late in range(2):
+            core_copy(late, r).wait_send()
         far_copy(r).wait_send()
         out_copy(r).wait()
 
@@ -416,22 +433,22 @@
             vmem((2, 2, 4, 2, 2, N, N), BF),
             vmem((4, 2, 2, 2, 8, N), F32),
             vmem((4, 2, 2, 2, 8, N), F32),
-            vmem((2, ATOMS, 2, N, N), BF),
-            vmem((2, ATOMS, 2, N, N), BF),
+            vmem((2, STEPS, ATOMS, 2, STRIP, N), BF),
+            vmem((2, STEPS, ATOMS, 2, STRIP, N), BF),
             vmem((STEPS, ATOMS, 2, STRIP, N), F32),
             vmem((STEPS, ATOMS, 2, STRIP, N), BF),
             vmem((STEPS, ATOMS, 2, STRIP, N), BF),
             vmem((STEPS, ATOMS, 2, STRIP, N), BF),
             smem((2, MODES, BONDS), F32), smem((MODES, BONDS), jnp.int32), smem((BONDS,), jnp.int32),
-            smem((OWNERS,), jnp.int32), smem((OWNERS,), jnp.int32), smem((OWNERS,), jnp.int32),
-            smem((OWNERS,), jnp.int32), smem((BONDS,), jnp.int32), smem((BONDS, 2 * MODES), F32),
+            smem((BONDS,), jnp.int32), smem((BONDS,), jnp.int32), smem((BONDS,), jnp.int32),
+            smem((OWNERS, 2), jnp.int32), smem((BONDS, 2 * MODES), F32),
             dma((3,)), dma((CHUNKS, PARTS)), dma((CHUNKS, PARTS)),
             dma((CHUNKS, 2)), dma((CHUNKS, 2)),
             dma((PAIRS, PARTS)), dma((PAIRS, PARTS)),
             dma, dma((PAIRS,)), dma,
             dma((4,)), dma((4,)),
             dma((2, 2, 4)), dma((2, 2, 4)),
-            dma((2,)), dma((2,)),
+            dma((2, STEPS)), dma((2, STEPS)),
             dma((STEPS,)), dma((STEPS,)), dma((STEPS,)),
         ],
         compiler_params=pltpu.CompilerParams(

time: 99.8 us -> 94.8 us (0.950)
  Pallas kernels: 97.5 us -> 92.8 us
    pallas_call x1, Pallas kernels: 97.5 us -> 92.8 us  [body(): pl.pallas_call(kernel, out_shape=jax.ShapeDtypeStruct((ATOMS, 2, N, N), B...]
where the time goes in v3:
time: 94.8 us; the launch traced here: 94.7 us
  Pallas kernels  92.8 us (98%)
  local copies, waits for them, and re-layouts  1.89 us (2%)
    pallas_call x1, Pallas kernels, body(): pl.pallas_call(kernel, out_shape=jax.ShapeDtypeStruct((ATOMS, 2, N, N), B...  92.8 us

profile of v3, /device:TPU:66, one launch (start us, length us, event | category | flops | bytes accessed | tf_op | source)
XLA Modules:
  0.0 94.7 jit_solution(14657804406612933421)
XLA Ops:
  0.0 92.8 %shard_map.55 = bf16[8,2,128,128]{3,2,1,0:T(8,128)(2,1)} custom-call(bf16[16,2,128,128]{3,2,1,0:T(8,128)(2,1)} %bitcast.7, bf16[16,3,2,128,128]{4,3,2,1,0:T(8,128)(2,1)} %coupling.1, f32[2,4,16]{2,1,0:T(4,128)} %bitcast.8, s32[4,16]{1,0:T(4,128)} %bitcast.9, s32[16]{0:T(128)} %bond_atom_in.1), custom_call_target="tpu_custom_call" | custom-call | tf_op jit(solution)/shard_map/pallas_call | solution.py:422
  92.8 1.9 %copy.8 = bf16[8,1,2,128,128]{4,3,2,1,0:T(8,128)(2,1)} copy(bf16[8,1,2,128,128]{4,3,2,1,0:T(8,128)(2,1)} %bitcast.6) | data formatting | bytes 1048576

commit v4 on v3

--- a/solution.py
+++ b/solution.py
@@ -141,74 +141,83 @@
     for q in range(WINDOW):
         for s in ORDER:
             in_copy(q, s).start()
-    for load in small:
-        load.wait()
-
-    @pl.loop(0, BONDS)
-    def _(b):
-        owner = lax.div(bond_atom[b], ATOMS)
-        turn = lax.rem(lax.div(owner, 4) + 4 - x, 4)
-        place = jnp.where(turn == 2, 0, jnp.where(turn == 1, 1, 2))
-        late = jnp.where(lax.rem(lax.div(owner, 2), 2) == zh, 8, 0)
-        kind = jnp.where(lax.rem(owner, 2) == co, 1, 0)
-        key_of[b] = late + jnp.where(turn == 0, 6 + kind, 3 * kind + place)
-        place_of[b] = b
-
-    @pl.loop(EARLY, BONDS)
-    def _(b):
-        mine = key_of[b] * BONDS + b
-        rank = jnp.int32(EARLY)
-        for other in range(EARLY, BONDS):
-            rank = rank + jnp.where(key_of[other] * BONDS + other < mine, 1, 0)
-        place_of[b] = rank
-
-    @pl.loop(0, BONDS)
-    def _(at):
-        found = jnp.int32(0)
-        for b in range(BONDS):
-            found = found + jnp.where(place_of[b] == at, b, 0)
-        bond_at[at] = found
-
-    for late in range(2):
-        for kind in range(2):
-            for s in range(4):
-                key = key_index(late, kind, s)
-                first = jnp.int32(BONDS)
-                last = jnp.int32(-1)
-                for b in range(BONDS):
-                    hit = key_of[b] == key
-                    first = jnp.minimum(first, jnp.where(hit, b, BONDS))
-                    last = jnp.maximum(last, jnp.where(hit, b, -1))
-                named = last >= 0
-                for slot, bond in enumerate((first, last)):
-                    bond = jnp.minimum(jnp.maximum(bond, 0), BONDS - 1)
-                    slot_at[key, slot] = jnp.where(named, place_of[bond], 0)
-                    atom = jnp.where(named, lax.rem(bond_atom[bond], ATOMS), -1)
-                    meta[s, late, kind, slot] = jnp.full((8, N), atom.astype(F32), F32)
-
-    @pl.loop(0, BONDS)
-    def _(at):
-        b = bond_at[at]
-        for d in range(1, MODES + 1):
-            below = jnp.float32(0)
-            above = jnp.float32(0)
-            for mode in range(MODES):
-                hit = offset[mode, b] == d
-                below = below + jnp.where(hit, weight[0, mode, b], jnp.float32(0))
-                above = above + jnp.where(hit, weight[1, mode, b], jnp.float32(0))
-            table[at, d - 1] = below
-            table[at, MODES + d - 1] = above
+    def find_keys():
+        for load in small:
+            load.wait()
+
+
+        @pl.loop(0, BONDS)
+        def _(b):
+            owner = lax.div(bond_atom[b], ATOMS)
+            turn = lax.rem(lax.div(owner, 4) + 4 - x, 4)
+            place = jnp.where(turn == 2, 0, jnp.where(turn == 1, 1, 2))
+            late = jnp.where(lax.rem(lax.div(owner, 2), 2) == zh, 8, 0)
+            kind = jnp.where(lax.rem(owner, 2) == co, 1, 0)
+            key_of[b] = late + jnp.where(turn == 0, 6 + kind, 3 * kind + place)
+            place_of[b] = b
+
+        @pl.loop(EARLY, BONDS)
+        def _(b):
+            mine = key_of[b] * BONDS + b
+            rank = jnp.int32(EARLY)
+            for other in range(EARLY, BONDS):
+                rank = rank + jnp.where(key_of[other] * BONDS + other < mine, 1, 0)
+            place_of[b] = rank
+
+    def find_bonds():
+        @pl.loop(0, BONDS)
+        def _(at):
+            found = jnp.int32(0)
+            for b in range(BONDS):
+                found = found + jnp.where(place_of[b] == at, b, 0)
+            bond_at[at] = found
+
+    def find_slots(lates):
+        for late in lates:
+            for kind in range(2):
+                for s in range(4):
+                    key = key_index(late, kind, s)
+                    first = jnp.int32(BONDS)
+                    last = jnp.int32(-1)
+                    for b in range(BONDS):
+                        hit = key_of[b] == key
+                        first = jnp.minimum(first, jnp.where(hit, b, BONDS))
+                        last = jnp.maximum(last, jnp.where(hit, b, -1))
+                    named = last >= 0
+                    for slot, bond in enumerate((first, last)):
+                        bond = jnp.minimum(jnp.maximum(bond, 0), BONDS - 1)
+                        slot_at[key, slot] = jnp.where(named, place_of[bond], 0)
+                        atom = jnp.where(named, lax.rem(bond_atom[bond], ATOMS), -1)
+                        meta[s, late, kind, slot] = jnp.full((8, N), atom.astype(F32), F32)
+
+    def find_factors():
+        @pl.loop(0, BONDS)
+        def _(at):
+            b = bond_at[at]
+            for d in range(1, MODES + 1):
+                below = jnp.float32(0)
+                above = jnp.float32(0)
+                for mode in range(MODES):
+                    hit = offset[mode, b] == d
+                    below = below + jnp.where(hit, weight[0, mode, b], jnp.float32(0))
+                    above = above + jnp.where(hit, weight[1, mode, b], jnp.float32(0))
+                table[at, d - 1] = below
+                table[at, MODES + d - 1] = above
 
     own_load.wait()
 
-    @pl.loop(0, CHUNKS - WINDOW)
-    def _(q):
+    tasks = (
+        find_keys, find_bonds, functools.partial(find_slots, (0,)), functools.partial(find_slots, (1,)), find_factors,
+    )
+    for q in range(CHUNKS - WINDOW):
         for s in range(1, PARTS):
             in_arrival(q, s).wait_recv()
         for s in ORDER:
             in_copy(q + WINDOW, s).start()
         row_copy(q, 0).start()
         row_copy(q, 1).start()
+        if q < len(tasks):
+            tasks[q]()
 
     for s in range(1, 4):
         meta_copy(s).start()

time: 94.8 us -> 94.8 us (level)
  no operation moved by 1% of the time
where the time goes in v4:
time: 94.8 us; the launch traced here: 94.7 us
  Pallas kernels  92.8 us (98%)
  local copies, waits for them, and re-layouts  1.89 us (2%)
    pallas_call x1, Pallas kernels, body(): pl.pallas_call(kernel, out_shape=jax.ShapeDtypeStruct((ATOMS, 2, N, N), B...  92.8 us

profile of v4, /device:TPU:66, one launch (start us, length us, event | category | flops | bytes accessed | tf_op | source)
XLA Modules:
  0.0 94.7 jit_solution(3511295843258747885)
XLA Ops:
  0.0 92.8 %shard_map.55 = bf16[8,2,128,128]{3,2,1,0:T(8,128)(2,1)} custom-call(bf16[16,2,128,128]{3,2,1,0:T(8,128)(2,1)} %bitcast.7, bf16[16,3,2,128,128]{4,3,2,1,0:T(8,128)(2,1)} %coupling.1, f32[2,4,16]{2,1,0:T(4,128)} %bitcast.8, s32[4,16]{1,0:T(4,128)} %bitcast.9, s32[16]{0:T(128)} %bond_atom_in.1), custom_call_target="tpu_custom_call" | custom-call | tf_op jit(solution)/shard_map/pallas_call | solution.py:431
  92.8 1.9 %copy.8 = bf16[8,1,2,128,128]{4,3,2,1,0:T(8,128)(2,1)} copy(bf16[8,1,2,128,128]{4,3,2,1,0:T(8,128)(2,1)} %bitcast.6) | data formatting | bytes 1048576
